TPU v7x, 128 devices: a whole 4x4x4 slice. The times are simulated.
128 devices in a mesh: slab: 8 (over y_hi, x), line: 16 (over z, y_lo, core).
Axes of the slice: x: 4, y: 4 (y_hi: 2, y_lo: 2; y = y_hi * 2 + y_lo), z: 4, core: 2. Of those that a mesh axis runs over, the one named last changes fastest.
Arguments:
- estimate: float32 [256, 256, 256], P('slab', 'line'), may hold values from -6 to 6
- support_lo: int32 [256, 256], P('slab', 'line'), may hold values from 0 to 63
- support_hi: int32 [256, 256], P('slab', 'line'), may hold values from 193 to 256
- measured: bfloat16 [2, 2, 512, 512, 2, 128], P(None, None, None, ('slab', 'line')), may hold values from -3 to 3
- blocks: int32 [512, 2, 2], replicated, may hold values from 0 to 3, all different within a row
- wedge: int32 [2], replicated, may hold values from 0 to 511
Outputs:
- updated: float32 [256, 256, 256], P('slab', 'line')
Inputs may be any that keep to these rules, and one draw needn't show every extreme that they name: The 2 entries of blocks for one plane frequency and group are distinct.
All inputs are finite; a program needn't handle non-finite values.
Results may differ from a plain program's by a relative error of at most 0.0071.
Values may be sent and summed in bfloat16 or wider, within the bound.
A program may use at most 128 MiB of HBM per device.

v0:
```python
import math
import jax
import jax.numpy as jnp
from jax import lax
from jax.sharding import PartitionSpec as P

N = 512


def phase_table(left_int, right_int, period):
    product = jnp.mod(left_int * right_int, period)
    angle = product.astype(jnp.float32) * (2.0 * math.pi / period)
    factor = 1.0 / math.sqrt(N)
    return (
        (jnp.cos(angle) * factor).astype(jnp.bfloat16),
        (jnp.sin(angle) * factor).astype(jnp.bfloat16),
    )


def contract(form, left_op, right_op):
    return jnp.einsum(form, left_op, right_op, preferred_element_type=jnp.float32)


def shards(estimate, support_lo, support_hi, measured, blocks, wedge):
    slab_count = lax.axis_size("slab")
    line_count = lax.axis_size("line")
    slab_index = lax.axis_index("slab")
    line_index = lax.axis_index("line")
    plane_rows, row_count, obj_len = estimate.shape
    half_freq = N // 2
    per_line = N // line_count
    per_device = per_line // slab_count
    per_slab = N // slab_count
    cell_coord = jnp.arange(obj_len, dtype=jnp.int32) - obj_len // 2
    local_order = jnp.arange(per_line, dtype=jnp.int32)
    plane_freq = (
        local_order // per_device * per_slab + line_index * per_device + local_order % per_device
    )
    plane_cos, slice_sine_table = phase_table(
        (plane_freq - half_freq)[:, None], cell_coord[None, :], N
    )
    cells = estimate.astype(jnp.bfloat16)
    zero_block = jnp.zeros((plane_rows, per_line, obj_len), jnp.float32)
    piece = lax.all_gather(cells, "line", axis=1, tiled=True)
    imag_a = zero_block
    real_a = contract("kx,zxy->zky", plane_cos, piece)
    imag_a = imag_a - contract("kx,zxy->zky", slice_sine_table, piece)
    real_b = contract("ky,zxy->zkx", plane_cos, piece)
    imag_b = -contract("ky,zxy->zkx", slice_sine_table, piece)
    real_a, imag_a, real_b, imag_b = (real_a, imag_a, real_b, imag_b)
    spectrum = jnp.stack([jnp.stack([real_a, imag_a]), jnp.stack([real_b, imag_b])]).astype(
        jnp.bfloat16
    )
    gathered = lax.all_to_all(spectrum, "slab", split_axis=3, concat_axis=2, tiled=True)
    own_freq = (
        slab_index * per_slab + line_index * per_device + jnp.arange(per_device, dtype=jnp.int32)
    )
    all_freq = jnp.arange(N, dtype=jnp.int32) - half_freq
    dz_cos, dz_sin = phase_table(all_freq[:, None], cell_coord[None, :], N)
    pen_re = (
        contract("az,gzkc->gakc", dz_cos, gathered[:, 0])
        + contract("az,gzkc->gakc", dz_sin, gathered[:, 1])
    ).astype(jnp.bfloat16)
    pen_im = (
        contract("az,gzkc->gakc", dz_cos, gathered[:, 1])
        - contract("az,gzkc->gakc", dz_sin, gathered[:, 0])
    ).astype(jnp.bfloat16)
    frac_cos, frac_sin = phase_table(
        (2 * (own_freq - half_freq))[:, None, None] * all_freq[None, :, None],
        cell_coord[None, None, :],
        N * N,
    )
    polar_re = contract("klc,gakc->gakl", frac_cos, pen_re) + contract(
        "klc,gakc->gakl", frac_sin, pen_im
    )
    polar_im = contract("klc,gakc->gakl", frac_cos, pen_im) - contract(
        "klc,gakc->gakl", frac_sin, pen_re
    )
    block_len = measured.shape[-1]
    nblocks = N // block_len
    block_ids = jnp.arange(nblocks, dtype=jnp.int32)
    indicator_matrix = (blocks[:, :, :, None] == block_ids).astype(jnp.bfloat16)
    covered = jnp.any(blocks[:, :, :, None] == block_ids, axis=2)
    overwritten_result = contract("voef,ozvnei->ozvnfi", indicator_matrix, measured)
    low_end = jnp.minimum(wedge[0], wedge[1])
    high_end = jnp.maximum(wedge[0], wedge[1])
    line_pos = jnp.arange(N, dtype=jnp.int32)
    excluded = ((line_pos >= low_end) & (line_pos < high_end)).reshape(nblocks, block_len)
    usable = (
        jnp.transpose(covered, (1, 0, 2))[:, :, None, :, None] & (~excluded)[None, None, None, :, :]
    )
    kweight = ((jnp.abs(own_freq - half_freq).astype(jnp.float32) + 1.0) / half_freq)[
        None, None, :, None, None
    ]
    shape_five = (2, N, per_device, nblocks, block_len)
    weighted_re = (
        (jnp.where(usable, overwritten_result[:, 0], polar_re.reshape(shape_five)) * kweight)
        .reshape(2, N, per_device, N)
        .astype(jnp.bfloat16)
    )
    weighted_im = (
        (jnp.where(usable, overwritten_result[:, 1], polar_im.reshape(shape_five)) * kweight)
        .reshape(2, N, per_device, N)
        .astype(jnp.bfloat16)
    )
    adj_re = (
        contract("klc,gakl->gakc", frac_cos, weighted_re)
        - contract("klc,gakl->gakc", frac_sin, weighted_im)
    ).astype(jnp.bfloat16)
    adj_im = (
        contract("klc,gakl->gakc", frac_cos, weighted_im)
        + contract("klc,gakl->gakc", frac_sin, weighted_re)
    ).astype(jnp.bfloat16)
    plan_re = (
        contract("az,gakc->gzkc", dz_cos, adj_re) - contract("az,gakc->gzkc", dz_sin, adj_im)
    ).astype(jnp.bfloat16)
    plan_im = (
        contract("az,gakc->gzkc", dz_cos, adj_im) + contract("az,gakc->gzkc", dz_sin, adj_re)
    ).astype(jnp.bfloat16)
    returned = lax.all_to_all(
        jnp.stack([plan_re, plan_im], axis=1), "slab", split_axis=2, concat_axis=3, tiled=True
    )
    partial_image = contract("kx,zky->zxy", plane_cos, returned[0, 0]) - contract(
        "kx,zky->zxy", slice_sine_table, returned[0, 1]
    )
    partial_image = (
        partial_image
        + contract("ky,zkx->zxy", plane_cos, returned[1, 0])
        - contract("ky,zkx->zxy", slice_sine_table, returned[1, 1])
    )
    summed = lax.psum_scatter(partial_image, "line", scatter_dimension=1, tiled=True)
    ycoord = jnp.arange(obj_len, dtype=jnp.int32)
    inside = (ycoord[None, None, :] >= support_lo[:, :, None]) & (
        ycoord[None, None, :] < support_hi[:, :, None]
    )
    return jnp.where(inside & (summed > 0.0), summed, jnp.float32(0.0))


def solution(mesh):
    in_specs = (
        P("slab", "line", None),
        P("slab", "line"),
        P("slab", "line"),
        P(None, None, None, ("slab", "line"), None, None),
        P(),
        P(),
    )
    out_specs = P("slab", "line", None)
    return jax.shard_map(shards, mesh=mesh, in_specs=in_specs, out_specs=out_specs, check_vma=False)
```

profile of v0, /device:TPU:0, one launch (start us, length us, event | category | flops | bytes accessed | tf_op | source)
XLA Modules:
  0.0 397.7 jit_solution(11599687042185202227)
XLA Ops:
  6.5 0.0 all-gather.2.cloned.1.call-start
  6.5 1.8 convert_element_type.109
  8.3 0.0 all-gather.2.cloned.1.call-update
  8.3 1.4 fusion.223
  12.2 0.9 copy.70
  13.2 12.0 %convolution_bitcast_fusion = f32[2,2,512,4,4,128]{5,4,3,1,2,0:T(4,128)} fusion(bf16[2,2,512,4,2,128]{5,4,3,2,1,0:T(2,128)(2,1)} %param.9, s32[512,2,2]{2,0,1:T(8,128)S(1)} %copy.70), kind=kOutput, calls=%fused_computation | convolution fusion | flops 16785408 | bytes 20979712 | tf_op jit(solution)/shard_map/voef,ozvnei->ozvnfi/dot_general | solution.py:21
  25.2 23.5 %all-gather.2.cloned.1.call-done = bf16[32,256,256]{2,1,0:T(8,128)(2,1)} async-done(((bf16[32,16,256]{2,1,0:T(8,128)(2,1)}), bf16[32,256,256]{2,1,0:T(8,128)(2,1)}) %all-gather.2.cloned.1.call-update) | async-done | bytes 4194320 | tf_op jit(solution)/shard_map/all_gather | solution.py:44
  48.8 3.3 fusion.43
  52.1 0.1 copy-done
  52.2 1.0 fusion.40
  53.2 1.4 fusion.42
  54.6 1.4 fusion.41
  56.0 0.2 maximum_bitcast_fusion
  56.2 0.2 pad_maximum_fusion
  56.4 2.5 copy.72
  58.9 6.5 %all-to-all-start = ((bf16[2,2,32,32,256]{4,2,1,0,3:T(8,128)(2,1)}), bf16[2,2,32,32,256]{4,2,1,0,3:T(8,128)(2,1)S(1)}, u32[]{:S(2)}, u32[]{:S(2)}) async-start(bf16[2,2,32,32,256]{4,2,1,0,3:T(8,128)(2,1)} %copy.72), calls=%async_computation | async-start | bytes 4194304 | tf_op jit(solution)/shard_map/all_to_all | solution.py:54
  65.4 0.5 reduce-scatter.2.cloned.1.call-start
  65.9 12.3 %fusion.222 = (f32[2,1,512,4,4,128]{5,4,3,1,2,0:T(4,128)}, f32[2,1,512,4,4,128]{5,4,3,1,2,0:T(4,128)}) fusion(f32[2,2,512,4,4,128]{5,4,3,1,2,0:T(4,128)} %convolution_bitcast_fusion), kind=kLoop, calls=%fused_computation.250 | loop fusion | bytes 33554432 | tf_op jit(solution)/shard_map/slice | solution.py:97
  78.2 10.6 %squeeze.33 = f32[2,512,4,512]{3,2,1,0:T(4,128)} reshape(f32[2,1,512,4,4,128]{5,4,3,1,2,0:T(4,128)} %get-tuple-element.6) | data formatting | bytes 16777216 | tf_op jit(solution)/shard_map/squeeze | solution.py:102
  88.8 5.8 %fusion.56 = pred[512,2,4]{2,0,1:T(8,128)(4,1)S(1)} fusion(s32[512,2,2]{2,0,1:T(8,128)S(1)} %copy.70), kind=kLoop, calls=%fused_computation.68 | loop fusion | flops 12288 | bytes 12288 | tf_op jit(solution)/shard_map/reduce_or | solution.py:83
  94.7 3.5 and.95
  98.1 0.5 and.96
  98.6 10.7 %squeeze.30 = f32[2,512,4,512]{3,2,1,0:T(4,128)} reshape(f32[2,1,512,4,4,128]{5,4,3,1,2,0:T(4,128)} %get-tuple-element.5) | data formatting | bytes 16777216 | tf_op jit(solution)/shard_map/squeeze | solution.py:97
  109.3 0.1 broadcast_multiply_fusion
  109.4 0.3 broadcast_and_fusion
  109.7 0.0 all-to-all-done
  109.7 0.2 copy.74
  109.9 2.7 fusion.58
  112.5 2.7 fusion.57
  115.2 3.1 fusion.25
  118.3 3.3 fusion.24
  121.6 0.0 slice-start
  121.6 11.8 %fusion.18 = f32[4,2,512,512]{3,2,1,0:T(8,128)} fusion(bf16[2,512,4,256]{1,3,2,0:T(8,128)(2,1)S(1)} %fusion.25, s32[256]{0:T(256)S(1)} %iota_add_fusion.1, s32[4,512]{1,0:T(4,128)S(1)} %broadcast_multiply_fusion), kind=kOutput, calls=%fused_computation.37 | convolution fusion | flops 1082130432 | bytes 10494976 | tf_op jit(solution)/shard_map/klc,gakc->gakl/dot_general | solution.py:21
  133.4 8.9 %fusion.22 = f32[4,2,512,512]{3,2,1,0:T(8,128)S(1)} fusion(bf16[2,512,4,256]{1,3,2,0:T(8,128)(2,1)S(1)} %fusion.24, s32[256]{0:T(256)S(1)} %iota_add_fusion.1, s32[4,512]{1,0:T(4,128)S(1)} %broadcast_multiply_fusion), kind=kOutput, calls=%fused_computation.41 | convolution fusion | flops 1082130432 | bytes 10494976 | tf_op jit(solution)/shard_map/klc,gakc->gakl/dot_general | solution.py:21
  142.3 0.0 slice-done
  142.3 0.0 slice-done.1
  142.4 0.0 slice-start.3
  142.4 15.3 %fusion.2 = bf16[2,512,4,512]{3,1,0,2:T(8,128)(2,1)} fusion(f32[2,512,4,512]{3,2,1,0:T(4,128)S(1)} %bitcast.156, f32[4,2,512,512]{3,2,1,0:T(8,128)} %fusion.18, f32[4]{0:T(128)S(1)} %add_multiply_fusion, pred[2,512,512]{2,1,0:T(8,128)(4,1)S(1)} %broadcast_and_fusion, bf16[2,512,4,256]{1,3,2,0:T(8,128)(2,1)S(1)} %fusion.24, s32[256]{0:T(256)S(1)} %iota_add_fusion.1, ...), kind=kOutput, calls=%fused_computation.5 | convolution fusion | flops 1090519040 | bytes 23602192 | tf_op jit(solution)/shard_map/klc,gakc->gakl/dot_general | solution.py:21
  157.7 12.2 %fusion.50 = f32[4,2,512,256]{3,2,1,0:T(8,128)} fusion(bf16[2,512,4,512]{3,1,0,2:T(8,128)(2,1)} %fusion.2, s32[256]{0:T(256)S(1)} %iota_add_fusion.1, s32[4,512]{1,0:T(4,128)S(1)} %broadcast_multiply_fusion), kind=kOutput, calls=%fused_computation.65 | convolution fusion | flops 1082130432 | bytes 8397824 | tf_op jit(solution)/shard_map/klc,gakl->gakc/dot_general | solution.py:21
  169.9 12.5 %fusion.4 = bf16[2,512,4,512]{3,1,0,2:T(8,128)(2,1)S(1)} fusion(f32[2,512,4,512]{3,2,1,0:T(4,128)S(1)} %bitcast.158, f32[4,2,512,512]{3,2,1,0:T(8,128)S(1)} %fusion.22, f32[4]{0:T(128)S(1)} %add_multiply_fusion, pred[2,512,512]{2,1,0:T(8,128)(4,1)S(1)} %broadcast_and_fusion, bf16[2,512,4,256]{1,3,2,0:T(8,128)(2,1)S(1)} %fusion.25, ...), kind=kOutput, calls=%fused_computation.8 | convolution fusion | flops 1090519040 | bytes 23602192 | tf_op jit(solution)/shard_map/klc,gakc->gakl/dot_general | solution.py:21
  182.5 8.5 %fusion.53 = f32[4,2,512,256]{3,2,1,0:T(8,128)S(1)} fusion(bf16[2,512,4,512]{3,1,0,2:T(8,128)(2,1)S(1)} %fusion.4, s32[256]{0:T(256)S(1)} %iota_add_fusion.1, s32[4,512]{1,0:T(4,128)S(1)} %broadcast_multiply_fusion), kind=kOutput, calls=%fused_computation.66 | convolution fusion | flops 1082130432 | bytes 8397824 | tf_op jit(solution)/shard_map/klc,gakl->gakc/dot_general | solution.py:21
  191.0 0.0 copy-done.4
  191.0 9.8 %fusion.27 = bf16[2,512,4,256]{3,1,0,2:T(8,128)(2,1)S(1)} fusion(f32[4,2,512,256]{3,2,1,0:T(8,128)S(1)} %copy-done.4, bf16[2,512,4,512]{3,1,0,2:T(8,128)(2,1)S(1)} %fusion.4, s32[256]{0:T(256)S(1)} %iota_add_fusion.1, s32[4,512]{1,0:T(4,128)S(1)} %broadcast_multiply_fusion), kind=kOutput, calls=%fused_computation.46 | convolution fusion | flops 1084227584 | bytes 10494976 | tf_op jit(solution)/shard_map/klc,gakl->gakc/dot_general | solution.py:21
  200.8 2.7 fusion.10
  203.5 2.7 fusion.12
  206.2 9.9 %fusion.26 = bf16[2,512,4,256]{3,1,0,2:T(8,128)(2,1)S(1)} fusion(f32[4,2,512,256]{3,2,1,0:T(8,128)S(1)} %fusion.53, bf16[2,512,4,512]{3,1,0,2:T(8,128)(2,1)S(1)} %copy-done.3, s32[256]{0:T(256)S(1)} %iota_add_fusion.1, s32[4,512]{1,0:T(4,128)S(1)} %broadcast_multiply_fusion), kind=kOutput, calls=%fused_computation.45 | convolution fusion | flops 1084227584 | bytes 10494976 | tf_op jit(solution)/shard_map/klc,gakl->gakc/dot_general | solution.py:21
  216.2 2.7 fusion.35
  218.9 2.7 fusion.32
  221.6 0.2 pad_maximum_fusion.1
  221.8 3.1 copy.87
  224.9 35.7 %all_to_all.36 = bf16[2,2,256,4,256]{4,3,0,1,2:T(4,128)(2,1)S(1)} all-to-all(bf16[2,2,256,4,256]{4,3,0,1,2:T(4,128)(2,1)} %copy.87), channel_id=1, replica_groups=mesh['slab'=8,'line'=16] {'slab'}, dimensions={2} | all-to-all | bytes 4194304 | tf_op jit(solution)/shard_map/all_to_all | solution.py:120
  260.7 0.7 copy.88
  261.4 3.0 copy.89
  264.4 2.5 all_to_all.33
  266.9 1.5 fusion.62
  268.4 1.4 fusion.64
  269.8 4.7 %fusion.63 = f32[32,256,256]{2,1,0:T(8,128)} fusion(bf16[2,2,32,32,256]{4,3,2,1,0:T(8,128)(2,1)S(1)} %all_to_all.33, s32[256]{0:T(256)S(1)} %iota_add_fusion.1, s32[32]{0:T(128)S(1)} %fusion.98), kind=kOutput, calls=%fused_computation.84 | convolution fusion | flops 134348800 | bytes 8914432 | tf_op jit(solution)/shard_map/kx,zky->zxy/dot_general | solution.py:21
  274.5 8.9 %fusion = f32[32,256,256]{1,2,0:T(8,128)} fusion(f32[32,256,256]{1,2,0:T(8,128)S(1)} %fusion.62, f32[32,256,256]{2,1,0:T(8,128)S(1)} %fusion.64, f32[32,256,256]{2,1,0:T(8,128)} %fusion.63, bf16[2,2,32,32,256]{4,3,2,1,0:T(8,128)(2,1)S(1)} %all_to_all.33, s32[256]{0:T(256)S(1)} %iota_add_fusion.1, s32[32]{0:T(128)S(1)} %fusion.98), kind=kOutput, calls=%fused_computation.2 | convolution fusion | flops 140640256 | bytes 34080256 | tf_op jit(solution)/shard_map/ky,zkx->zxy/dot_general | solution.py:21
  283.4 10.3 %copy.92 = f32[32,256,256]{2,0,1:T(8,128)} copy(f32[32,256,256]{1,2,0:T(8,128)} %fusion) | data formatting | bytes 16777216 | tf_op jit(solution)/shard_map/sub | solution.py:127
  293.7 0.0 reduce-scatter.2.cloned.1.call-update
  293.8 94.5 %reduce-scatter.2.cloned.1.call-done = f32[32,16,256]{2,0,1:T(8,128)} async-done(((f32[32,256,256]{2,0,1:T(8,128)}), f32[32,16,256]{2,0,1:T(8,128)}) %reduce-scatter.2.cloned.1.call-update) | async-done | bytes 524304 | tf_op jit(solution)/shard_map/reduce_scatter | solution.py:131
  388.2 0.0 copy-done.1
  388.2 1.2 fusion.68
  389.5 1.1 copy.93
  (19 shorter events, 0.1 us)
Async XLA Ops:
  6.5 42.2 %all-gather.2.cloned.1.call-start = ((), (), s32[]{:S(2)}) async-start(), calls=%async_computation.3 | async-start | bytes 4456448 | tf_op jit(solution)/shard_map/all_gather | solution.py:44
  48.8 3.4 copy-start
  58.9 50.8 %all-to-all-start = ((bf16[2,2,32,32,256]{4,2,1,0,3:T(8,128)(2,1)}), bf16[2,2,32,32,256]{4,2,1,0,3:T(8,128)(2,1)S(1)}, u32[]{:S(2)}, u32[]{:S(2)}) async-start(bf16[2,2,32,32,256]{4,2,1,0,3:T(8,128)(2,1)} %copy.72), calls=%async_computation | async-start | bytes 4194304 | tf_op jit(solution)/shard_map/all_to_all | solution.py:54
  65.4 322.8 %reduce-scatter.2.cloned.1.call-start = ((), (), s32[]{:S(2)}) async-start(), calls=%async_computation.4 | async-start | bytes 8912896 | tf_op jit(solution)/shard_map/reduce_scatter | solution.py:131
  121.6 20.7 %slice-start = ((s8[8388608]{0:T(1024)(128)(4,1)}), s8[4194304]{0:T(1024)(128)(4,1)S(1)}, s32[]{:S(2)}) async-start(s8[8388608]{0:T(1024)(128)(4,1)} %bitcast.155), calls=%async_computation.5 | async-start | bytes 8388608
  133.4 8.9 %slice-start.1 = ((s8[8388608]{0:T(1024)(128)(4,1)}), s8[4194304]{0:T(1024)(128)(4,1)S(1)}, s32[]{:S(2)}) async-start(s8[8388608]{0:T(1024)(128)(4,1)} %bitcast.155), calls=%async_computation.6 | async-start | bytes 8388608
  133.4 36.5 %slice-start.2 = ((s8[8388608]{0:T(1024)(128)(4,1)}), s8[4194304]{0:T(1024)(128)(4,1)S(1)}, s32[]{:S(2)}) async-start(s8[8388608]{0:T(1024)(128)(4,1)} %bitcast.157), calls=%async_computation.7 | async-start | bytes 8388608
  142.4 27.6 %slice-start.3 = ((s8[8388608]{0:T(1024)(128)(4,1)}), s8[4194304]{0:T(1024)(128)(4,1)S(1)}, s32[]{:S(2)}) async-start(s8[8388608]{0:T(1024)(128)(4,1)} %bitcast.157), calls=%async_computation.8 | async-start | bytes 8388608
  182.5 8.5 %copy-start.4 = (f32[4,2,512,256]{3,2,1,0:T(8,128)S(1)}, f32[4,2,512,256]{3,2,1,0:T(8,128)}, u32[]{:S(2)}) copy-start(f32[4,2,512,256]{3,2,1,0:T(8,128)} %fusion.50) | copy-start | bytes 12582916
  203.5 2.7 copy-start.3
  293.7 94.5 %copy-start.1 = (s32[32,16]{0,1:T(8,128)S(1)}, s32[32,16]{0,1:T(8,128)}, u32[]{:S(2)}) copy-start(s32[32,16]{0,1:T(8,128)} %param.8) | copy-start | bytes 6148
  293.7 94.5 %copy-start.2 = (s32[32,16]{0,1:T(8,128)S(1)}, s32[32,16]{0,1:T(8,128)}, u32[]{:S(2)}) copy-start(s32[32,16]{0,1:T(8,128)} %param.7) | copy-start | bytes 6148
Sparse Core Ops, SparseCore 0:
  9.0 39.7 all-gather.1
  293.9 94.2 reduce-scatter.1
where the time goes:
time: 404 us; the launch traced here: 398 us
  matrix products  147 us (36%)
  waiting for transfers between devices  118 us (29%)
  local copies, waits for them, and re-layouts  63.4 us (16%)
  blocking collectives  35.7 us (9%)
  between operations  16.5 us (4%)
  other arithmetic  9.83 us (2%)
  starting transfers between devices  7.02 us (2%)
    dot_general x25, matrix products, contract(): jnp.einsum(form, left_op, right_op, preferred_element_type=jnp.float32)  147 us
    reduce_scatter x1, waiting for transfers between devices, shards(): lax.psum_scatter(partial_image, 'line', scatter_dimension=1, tiled=True)  94.5 us
    all_to_all x1, blocking collectives, shards(): lax.all_to_all(jnp.stack([plan_re, plan_im], axis=1), 'slab', split_axis=...  35.7 us
    all_gather x1, waiting for transfers between devices, shards(): piece = lax.all_gather(cells, 'line', axis=1, tiled=True)  23.5 us
    slice x1, local copies, waits for them, and re-layouts, shards(): overwritten_result[:, 0]  12.3 us
    squeeze x1, local copies, waits for them, and re-layouts, shards(): overwritten_result[:, 0]  10.7 us
    squeeze x1, local copies, waits for them, and re-layouts, shards(): overwritten_result[:, 1]  10.6 us
    sub x1, local copies, waits for them, and re-layouts, shards(): partial_image + contract('ky,zkx->zxy', plane_cos, returned[1, 0])  10.3 us
  transfers between devices with their start and end apart: 3, of which 2 were waited for; matrix products, arithmetic and copies ran while one was open for 15% of the time, Pallas kernels for 0%

commit v1 on v0

--- a/solution.py
+++ b/solution.py
@@ -3,6 +3,7 @@
 import jax.numpy as jnp
 from jax import lax
 from jax.sharding import PartitionSpec as P
+from jax.lax import all_to_all, axis_size
 
 N = 512
 
@@ -41,7 +42,9 @@
     )
     cells = estimate.astype(jnp.bfloat16)
     zero_block = jnp.zeros((plane_rows, per_line, obj_len), jnp.float32)
-    piece = lax.all_gather(cells, "line", axis=1, tiled=True)
+    piece = jnp.concatenate(
+        all_to_all(jnp.stack([cells for _ in range(axis_size("line"))]), "line", 0, 0), axis=1
+    )
     imag_a = zero_block
     real_a = contract("kx,zxy->zky", plane_cos, piece)
     imag_a = imag_a - contract("kx,zxy->zky", slice_sine_table, piece)

time: 404 us -> 422 us (1.045)
  waiting for transfers between devices: 118 us -> 129 us
  starting transfers between devices: 7.02 us -> 13.9 us
    all_to_all x0 -> x1, waiting for transfers between devices: none -> 34.9 us  [shards(): all_to_all(jnp.stack([cells for _ in range(axis_size('line'))]), 'line',...]
    all_gather x1 -> x0, waiting for transfers between devices: 23.5 us -> none  [shards(): piece = lax.all_gather(cells, 'line', axis=1, tiled=True)]
    all_to_all x0 -> x1, starting transfers between devices: none -> 6.72 us  [shards(): all_to_all(jnp.stack([cells for _ in range(axis_size('line'))]), 'line',...]
  transfers between devices with their start and end apart: 3 -> 3, of which waited for: 2 -> 2; matrix products, arithmetic and copies ran while one was open for 15% -> 14% of each run, Pallas kernels for 0% -> 0%
where the time goes in v1:
time: 422 us; the launch traced here: 415 us
  matrix products  145 us (34%)
  waiting for transfers between devices  129 us (31%)
  local copies, waits for them, and re-layouts  66.9 us (16%)
  blocking collectives  35 us (8%)
  between operations  16.5 us (4%)
  starting transfers between devices  13.9 us (3%)
  other arithmetic  9.13 us (2%)
    dot_general x25, matrix products, contract(): jnp.einsum(form, left_op, right_op, preferred_element_type=jnp.float32)  145 us
    reduce_scatter x1, waiting for transfers between devices, shards(): lax.psum_scatter(partial_image, 'line', scatter_dimension=1, tiled=True)  93.7 us
    all_to_all x1, blocking collectives, shards(): lax.all_to_all(jnp.stack([plan_re, plan_im], axis=1), 'slab', split_axis=...  35 us
    all_to_all x1, waiting for transfers between devices, shards(): all_to_all(jnp.stack([cells for _ in range(axis_size('line'))]), 'line',...  34.9 us
    slice x1, local copies, waits for them, and re-layouts, shards(): overwritten_result[:, 0]  12.3 us
    squeeze x1, local copies, waits for them, and re-layouts, shards(): overwritten_result[:, 0]  10.7 us
    squeeze x1, local copies, waits for them, and re-layouts, shards(): overwritten_result[:, 1]  10.6 us
    sub x1, local copies, waits for them, and re-layouts, shards(): partial_image + contract('ky,zkx->zxy', plane_cos, returned[1, 0])  10.3 us
  transfers between devices with their start and end apart: 3, of which 2 were waited for; matrix products, arithmetic and copies ran while one was open for 14% of the time, Pallas kernels for 0%

profile of v1, /device:TPU:0, one launch (start us, length us, event | category | flops | bytes accessed | tf_op | source)
XLA Modules:
  0.0 415.0 jit_solution(16227959412307347791)
XLA Ops:
  6.5 1.1 convert_element_type.109
  7.6 2.4 stack.64
  10.0 6.7 %all-to-all-start = ((bf16[16,32,16,256]{3,2,1,0:T(8,128)(2,1)}), bf16[16,32,16,256]{3,2,1,0:T(8,128)(2,1)}, u32[]{:S(2)}, u32[]{:S(2)}) async-start(bf16[16,32,16,256]{3,2,1,0:T(8,128)(2,1)} %stack.64), calls=%async_computation | async-start | bytes 8388608 | tf_op jit(solution)/shard_map/all_to_all | solution.py:46
  16.8 0.6 fusion.223
  19.9 0.0 copy-done
  19.9 0.2 copy.71
  20.1 12.0 %convolution_bitcast_fusion = f32[2,2,512,4,4,128]{5,4,3,1,2,0:T(4,128)} fusion(bf16[2,2,512,4,2,128]{5,4,3,2,1,0:T(2,128)(2,1)} %param.9, s32[512,2,2]{2,0,1:T(8,128)S(1)} %copy.71), kind=kOutput, calls=%fused_computation | convolution fusion | flops 16785408 | bytes 20979712 | tf_op jit(solution)/shard_map/voef,ozvnei->ozvnfi/dot_general | solution.py:22
  32.2 34.9 %all-to-all-done = bf16[16,32,16,256]{3,2,1,0:T(8,128)(2,1)} async-done(((bf16[16,32,16,256]{3,2,1,0:T(8,128)(2,1)}), bf16[16,32,16,256]{3,2,1,0:T(8,128)(2,1)}, u32[]{:S(2)}, u32[]{:S(2)}) %all-to-all-start) | async-done | bytes 4194336 | tf_op jit(solution)/shard_map/all_to_all | solution.py:46
  67.1 2.7 copy.73
  69.8 1.0 fusion.43
  70.8 1.0 fusion.40
  71.8 1.4 fusion.42
  73.2 1.4 fusion.41
  74.6 0.2 maximum_bitcast_fusion
  74.8 0.2 pad_maximum_fusion
  75.0 2.5 copy.74
  77.5 6.6 %all-to-all-start.1 = ((bf16[2,2,32,32,256]{4,2,1,0,3:T(8,128)(2,1)}), bf16[2,2,32,32,256]{4,2,1,0,3:T(8,128)(2,1)S(1)}, u32[]{:S(2)}, u32[]{:S(2)}) async-start(bf16[2,2,32,32,256]{4,2,1,0,3:T(8,128)(2,1)} %copy.74), calls=%async_computation.1 | async-start | bytes 4194304 | tf_op jit(solution)/shard_map/all_to_all | solution.py:57
  84.2 0.5 reduce-scatter.2.cloned.1.call-start
  84.7 12.3 %fusion.222 = (f32[2,1,512,4,4,128]{5,4,3,1,2,0:T(4,128)}, f32[2,1,512,4,4,128]{5,4,3,1,2,0:T(4,128)}) fusion(f32[2,2,512,4,4,128]{5,4,3,1,2,0:T(4,128)} %convolution_bitcast_fusion), kind=kLoop, calls=%fused_computation.250 | loop fusion | bytes 33554432 | tf_op jit(solution)/shard_map/slice | solution.py:100
  96.9 10.6 %squeeze.33 = f32[2,512,4,512]{3,2,1,0:T(4,128)} reshape(f32[2,1,512,4,4,128]{5,4,3,1,2,0:T(4,128)} %get-tuple-element.6) | data formatting | bytes 16777216 | tf_op jit(solution)/shard_map/squeeze | solution.py:105
  107.6 5.8 %fusion.56 = pred[512,2,4]{2,0,1:T(8,128)(4,1)S(1)} fusion(s32[512,2,2]{2,0,1:T(8,128)S(1)} %copy.71), kind=kLoop, calls=%fused_computation.68 | loop fusion | flops 12288 | bytes 12288 | tf_op jit(solution)/shard_map/reduce_or | solution.py:86
  113.4 3.5 and.95
  116.9 0.5 and.96
  117.4 10.7 %squeeze.30 = f32[2,512,4,512]{3,2,1,0:T(4,128)} reshape(f32[2,1,512,4,4,128]{5,4,3,1,2,0:T(4,128)} %get-tuple-element.5) | data formatting | bytes 16777216 | tf_op jit(solution)/shard_map/squeeze | solution.py:100
  128.1 0.1 broadcast_multiply_fusion
  128.1 0.3 broadcast_and_fusion
  128.4 0.0 all-to-all-done.1
  128.4 0.2 copy.76
  128.6 2.7 fusion.58
  131.3 2.7 fusion.57
  133.9 3.1 fusion.25
  137.0 3.3 fusion.24
  140.3 0.0 slice-start
  140.3 11.8 %fusion.18 = f32[4,2,512,512]{3,2,1,0:T(8,128)} fusion(bf16[2,512,4,256]{1,3,2,0:T(8,128)(2,1)S(1)} %fusion.25, s32[256]{0:T(256)S(1)} %iota_add_fusion.1, s32[4,512]{1,0:T(4,128)S(1)} %broadcast_multiply_fusion), kind=kOutput, calls=%fused_computation.37 | convolution fusion | flops 1082130432 | bytes 10494976 | tf_op jit(solution)/shard_map/klc,gakc->gakl/dot_general | solution.py:22
  152.2 8.9 %fusion.22 = f32[4,2,512,512]{3,2,1,0:T(8,128)S(1)} fusion(bf16[2,512,4,256]{1,3,2,0:T(8,128)(2,1)S(1)} %fusion.24, s32[256]{0:T(256)S(1)} %iota_add_fusion.1, s32[4,512]{1,0:T(4,128)S(1)} %broadcast_multiply_fusion), kind=kOutput, calls=%fused_computation.41 | convolution fusion | flops 1082130432 | bytes 10494976 | tf_op jit(solution)/shard_map/klc,gakc->gakl/dot_general | solution.py:22
  161.1 0.0 slice-done
  161.1 0.0 slice-done.1
  161.1 0.0 slice-start.3
  161.1 15.3 %fusion.2 = bf16[2,512,4,512]{3,1,0,2:T(8,128)(2,1)} fusion(f32[2,512,4,512]{3,2,1,0:T(4,128)S(1)} %bitcast.162, f32[4,2,512,512]{3,2,1,0:T(8,128)} %fusion.18, f32[4]{0:T(128)S(1)} %add_multiply_fusion, pred[2,512,512]{2,1,0:T(8,128)(4,1)S(1)} %broadcast_and_fusion, bf16[2,512,4,256]{1,3,2,0:T(8,128)(2,1)S(1)} %fusion.24, s32[256]{0:T(256)S(1)} %iota_add_fusion.1, ...), kind=kOutput, calls=%fused_computation.5 | convolution fusion | flops 1090519040 | bytes 23602192 | tf_op jit(solution)/shard_map/klc,gakc->gakl/dot_general | solution.py:22
  176.4 12.2 %fusion.50 = f32[4,2,512,256]{3,2,1,0:T(8,128)} fusion(bf16[2,512,4,512]{3,1,0,2:T(8,128)(2,1)} %fusion.2, s32[256]{0:T(256)S(1)} %iota_add_fusion.1, s32[4,512]{1,0:T(4,128)S(1)} %broadcast_multiply_fusion), kind=kOutput, calls=%fused_computation.65 | convolution fusion | flops 1082130432 | bytes 8397824 | tf_op jit(solution)/shard_map/klc,gakl->gakc/dot_general | solution.py:22
  188.7 0.0 slice-done.2
  188.7 12.5 %fusion.4 = bf16[2,512,4,512]{3,1,0,2:T(8,128)(2,1)S(1)} fusion(f32[2,512,4,512]{3,2,1,0:T(4,128)S(1)} %bitcast.164, f32[4,2,512,512]{3,2,1,0:T(8,128)S(1)} %fusion.22, f32[4]{0:T(128)S(1)} %add_multiply_fusion, pred[2,512,512]{2,1,0:T(8,128)(4,1)S(1)} %broadcast_and_fusion, bf16[2,512,4,256]{1,3,2,0:T(8,128)(2,1)S(1)} %fusion.25, ...), kind=kOutput, calls=%fused_computation.8 | convolution fusion | flops 1090519040 | bytes 23602192 | tf_op jit(solution)/shard_map/klc,gakc->gakl/dot_general | solution.py:22
  201.2 8.5 %fusion.53 = f32[4,2,512,256]{3,2,1,0:T(8,128)S(1)} fusion(bf16[2,512,4,512]{3,1,0,2:T(8,128)(2,1)S(1)} %fusion.4, s32[256]{0:T(256)S(1)} %iota_add_fusion.1, s32[4,512]{1,0:T(4,128)S(1)} %broadcast_multiply_fusion), kind=kOutput, calls=%fused_computation.66 | convolution fusion | flops 1082130432 | bytes 8397824 | tf_op jit(solution)/shard_map/klc,gakl->gakc/dot_general | solution.py:22
  209.7 9.8 %fusion.27 = bf16[2,512,4,256]{3,1,0,2:T(8,128)(2,1)S(1)} fusion(f32[4,2,512,256]{3,2,1,0:T(8,128)S(1)} %copy-done.5, bf16[2,512,4,512]{3,1,0,2:T(8,128)(2,1)S(1)} %fusion.4, s32[256]{0:T(256)S(1)} %iota_add_fusion.1, s32[4,512]{1,0:T(4,128)S(1)} %broadcast_multiply_fusion), kind=kOutput, calls=%fused_computation.46 | convolution fusion | flops 1084227584 | bytes 10494976 | tf_op jit(solution)/shard_map/klc,gakl->gakc/dot_general | solution.py:22
  219.6 2.7 fusion.10
  222.3 2.7 fusion.12
  225.0 9.9 %fusion.26 = bf16[2,512,4,256]{3,1,0,2:T(8,128)(2,1)S(1)} fusion(f32[4,2,512,256]{3,2,1,0:T(8,128)S(1)} %fusion.53, bf16[2,512,4,512]{3,1,0,2:T(8,128)(2,1)S(1)} %copy-done.4, s32[256]{0:T(256)S(1)} %iota_add_fusion.1, s32[4,512]{1,0:T(4,128)S(1)} %broadcast_multiply_fusion), kind=kOutput, calls=%fused_computation.45 | convolution fusion | flops 1084227584 | bytes 10494976 | tf_op jit(solution)/shard_map/klc,gakl->gakc/dot_general | solution.py:22
  234.9 2.7 fusion.35
  237.6 2.7 fusion.32
  240.4 0.2 pad_maximum_fusion.1
  240.6 3.1 copy.89
  243.7 35.0 %all_to_all.41 = bf16[2,2,256,4,256]{4,3,0,1,2:T(4,128)(2,1)S(1)} all-to-all(bf16[2,2,256,4,256]{4,3,0,1,2:T(4,128)(2,1)} %copy.89), channel_id=1, replica_groups=mesh['slab'=8,'line'=16] {'slab'}, dimensions={2} | all-to-all | bytes 4194304 | tf_op jit(solution)/shard_map/all_to_all | solution.py:123
  278.7 0.7 copy.90
  279.4 3.0 copy.91
  282.4 2.5 all_to_all.37
  285.0 1.5 fusion.62
  286.5 1.4 fusion.64
  287.9 4.7 %fusion.63 = f32[32,256,256]{2,1,0:T(8,128)} fusion(bf16[2,2,32,32,256]{4,3,2,1,0:T(8,128)(2,1)S(1)} %all_to_all.37, s32[256]{0:T(256)S(1)} %iota_add_fusion.1, s32[32]{0:T(128)S(1)} %fusion.98), kind=kOutput, calls=%fused_computation.84 | convolution fusion | flops 134348800 | bytes 8914432 | tf_op jit(solution)/shard_map/kx,zky->zxy/dot_general | solution.py:22
  292.6 8.9 %fusion = f32[32,256,256]{1,2,0:T(8,128)} fusion(f32[32,256,256]{1,2,0:T(8,128)S(1)} %fusion.62, f32[32,256,256]{2,1,0:T(8,128)S(1)} %fusion.64, f32[32,256,256]{2,1,0:T(8,128)} %fusion.63, bf16[2,2,32,32,256]{4,3,2,1,0:T(8,128)(2,1)S(1)} %all_to_all.37, s32[256]{0:T(256)S(1)} %iota_add_fusion.1, s32[32]{0:T(128)S(1)} %fusion.98), kind=kOutput, calls=%fused_computation.2 | convolution fusion | flops 140640256 | bytes 34080256 | tf_op jit(solution)/shard_map/ky,zkx->zxy/dot_general | solution.py:22
  301.5 10.3 %copy.94 = f32[32,256,256]{2,0,1:T(8,128)} copy(f32[32,256,256]{1,2,0:T(8,128)} %fusion) | data formatting | bytes 16777216 | tf_op jit(solution)/shard_map/sub | solution.py:130
  311.8 0.0 reduce-scatter.2.cloned.1.call-update
  311.8 93.7 %reduce-scatter.2.cloned.1.call-done = f32[32,16,256]{2,0,1:T(8,128)} async-done(((f32[32,256,256]{2,0,1:T(8,128)}), f32[32,16,256]{2,0,1:T(8,128)}) %reduce-scatter.2.cloned.1.call-update) | async-done | bytes 524304 | tf_op jit(solution)/shard_map/reduce_scatter | solution.py:134
  405.5 1.2 fusion.68
  406.7 1.1 copy.95
  (22 shorter events, 0.1 us)
Async XLA Ops:
  10.0 6.7 %copy-start.3 = (s32[2]{0:T(128)S(1)}, s32[2]{0:T(128)}, u32[]{:S(2)}) copy-start(s32[2]{0:T(128)} %param.11) | copy-start | bytes 28
  10.0 9.9 %copy-start = (s32[512,2,2]{0,2,1:T(2,128)S(1)}, s32[512,2,2]{0,2,1:T(2,128)}, u32[]{:S(2)}) copy-start(s32[512,2,2]{0,2,1:T(2,128)} %param.10) | copy-start | bytes 24580
  10.0 57.1 %all-to-all-start = ((bf16[16,32,16,256]{3,2,1,0:T(8,128)(2,1)}), bf16[16,32,16,256]{3,2,1,0:T(8,128)(2,1)}, u32[]{:S(2)}, u32[]{:S(2)}) async-start(bf16[16,32,16,256]{3,2,1,0:T(8,128)(2,1)} %stack.64), calls=%async_computation | async-start | bytes 8388608 | tf_op jit(solution)/shard_map/all_to_all | solution.py:46
  77.5 50.9 %all-to-all-start.1 = ((bf16[2,2,32,32,256]{4,2,1,0,3:T(8,128)(2,1)}), bf16[2,2,32,32,256]{4,2,1,0,3:T(8,128)(2,1)S(1)}, u32[]{:S(2)}, u32[]{:S(2)}) async-start(bf16[2,2,32,32,256]{4,2,1,0,3:T(8,128)(2,1)} %copy.74), calls=%async_computation.1 | async-start | bytes 4194304 | tf_op jit(solution)/shard_map/all_to_all | solution.py:57
  84.2 321.3 %reduce-scatter.2.cloned.1.call-start = ((), (), s32[]{:S(2)}) async-start(), calls=%async_computation.4 | async-start | bytes 8912896 | tf_op jit(solution)/shard_map/reduce_scatter | solution.py:134
  140.3 20.7 %slice-start = ((s8[8388608]{0:T(1024)(128)(4,1)}), s8[4194304]{0:T(1024)(128)(4,1)S(1)}, s32[]{:S(2)}) async-start(s8[8388608]{0:T(1024)(128)(4,1)} %bitcast.161), calls=%async_computation.5 | async-start | bytes 8388608
  152.2 8.9 %slice-start.1 = ((s8[8388608]{0:T(1024)(128)(4,1)}), s8[4194304]{0:T(1024)(128)(4,1)S(1)}, s32[]{:S(2)}) async-start(s8[8388608]{0:T(1024)(128)(4,1)} %bitcast.161), calls=%async_computation.6 | async-start | bytes 8388608
  152.2 36.5 %slice-start.2 = ((s8[8388608]{0:T(1024)(128)(4,1)}), s8[4194304]{0:T(1024)(128)(4,1)S(1)}, s32[]{:S(2)}) async-start(s8[8388608]{0:T(1024)(128)(4,1)} %bitcast.163), calls=%async_computation.7 | async-start | bytes 8388608
  161.1 27.6 %slice-start.3 = ((s8[8388608]{0:T(1024)(128)(4,1)}), s8[4194304]{0:T(1024)(128)(4,1)S(1)}, s32[]{:S(2)}) async-start(s8[8388608]{0:T(1024)(128)(4,1)} %bitcast.163), calls=%async_computation.8 | async-start | bytes 8388608
  201.2 8.5 %copy-start.5 = (f32[4,2,512,256]{3,2,1,0:T(8,128)S(1)}, f32[4,2,512,256]{3,2,1,0:T(8,128)}, u32[]{:S(2)}) copy-start(f32[4,2,512,256]{3,2,1,0:T(8,128)} %fusion.50) | copy-start | bytes 12582916
  222.3 2.7 copy-start.4
  311.8 93.7 %copy-start.1 = (s32[32,16]{0,1:T(8,128)S(1)}, s32[32,16]{0,1:T(8,128)}, u32[]{:S(2)}) copy-start(s32[32,16]{0,1:T(8,128)} %param.8) | copy-start | bytes 6148
  311.8 93.7 %copy-start.2 = (s32[32,16]{0,1:T(8,128)S(1)}, s32[32,16]{0,1:T(8,128)}, u32[]{:S(2)}) copy-start(s32[32,16]{0,1:T(8,128)} %param.7) | copy-start | bytes 6148
Sparse Core Ops, SparseCore 0:
  311.9 93.5 reduce-scatter.1
